TPU v7x, 128 devices: a whole 4x4x4 slice. The times are simulated.
128 devices in a mesh: req: 16 (over z, y), kv: 8 (over x, core).
Axes of the slice: x: 4, y: 4, z: 4, core: 2. Of those that a mesh axis runs over, the one named last changes fastest.
Arguments:
- hidden_in: bfloat16 [16384, 2048], P(('req', 'kv')), may hold values from -6 to 6
- slot_tokens: int32 [16384], replicated, may hold values from 0 to 16383, as said below
- cache_len: int32 [128], P('req'), may hold values from 1 to 2048, 65536 in all
- prefill_start: int32 [16], P('req'), may hold values from 0 to 2048
- key_cache: bfloat16 [128, 2048, 1024], P('req', None, 'kv')
- value_cache: bfloat16 [128, 2048, 1024], P('req', None, 'kv'), may hold values from -18 to 18
- key_prefix: bfloat16 [16, 2048, 1024], P('req', None, 'kv')
- value_prefix: bfloat16 [16, 2048, 1024], P('req', None, 'kv'), may hold values from -18 to 18
- attn_gain: float32 [2048], replicated, may hold values from 0.25 to 1.75
- q_proj: bfloat16 [2048, 2048], P(None, 'kv'), may hold values from -0.125 to 0.125
- k_proj: bfloat16 [2048, 1024], P(None, 'kv'), may hold values from -0.125 to 0.125
- v_proj: bfloat16 [2048, 1024], P(None, 'kv'), may hold values from -0.125 to 0.125
- q_gain: float32 [128], replicated, may hold values from 0.25 to 1.75
- k_gain: float32 [128], replicated, may hold values from 0.25 to 1.75
- o_proj: bfloat16 [2048, 2048], P('kv'), may hold values from -0.125 to 0.125
- ffn_gain: float32 [2048], replicated, may hold values from 0.25 to 1.75
- w_gate: bfloat16 [2048, 6144], P(None, 'req'), may hold values from -0.125 to 0.125
- w_up: bfloat16 [2048, 6144], P(None, 'req'), may hold values from -0.125 to 0.125
- w_down: bfloat16 [6144, 2048], P('req'), may hold values from -0.078125 to 0.078125
- final_gain: float32 [2048], replicated, may hold values from 0.25 to 1.75
- lm_head: bfloat16 [2048, 151936], P(None, ('req', 'kv')), may hold values from -0.375 to 0.375
Outputs:
- layer_out: bfloat16 [16384, 2048], P(('req', 'kv'))
- max_logit: float32 [144], replicated
Inputs may be any that keep to these rules, and one draw needn't show every extreme that they name: slot_tokens is a permutation of the batch's tokens; each device's 128 consecutive slots take exactly 1 token from each device's 128 consecutive batch tokens.
All inputs are finite; a program needn't handle non-finite values. No bound on the sum of `cache_len` on one device may be relied on, other than what follows from the above.
Results may differ from a plain program's by a relative error of at most 0.0085.
The roundings to bfloat16 on the way count: a program that leaves them out, or rounds other values in their place, can miss the bound.
Values may be sent and summed in bfloat16 or wider, within the bound.
A program may use at most 128 MiB of HBM per device.

v0:
```python
import jax
import jax.numpy as jnp
from jax import lax
from jax.sharding import PartitionSpec as P

EPS = 1e-06
NEG = -1e30


def spread(value, axis, root):
    mine = lax.axis_index(axis) == root
    return lax.psum(jnp.where(mine, value, jnp.zeros_like(value)), axis)


def norm_rows(values, gain_vec):
    wide = values.astype(jnp.float32)
    return wide * lax.rsqrt(jnp.mean(wide * wide, axis=-1, keepdims=True) + EPS) * gain_vec


def rotate(values, places):
    half_dim = values.shape[-1] // 2
    freqs = 1000000.0 ** (-(jnp.arange(half_dim, dtype=jnp.float32) * 2.0 / values.shape[-1]))
    angles = places[:, None] * freqs[None, :]
    cosine = jnp.cos(angles)[:, None, :]
    sine = jnp.sin(angles)[:, None, :]
    first_half = values[..., :half_dim]
    second_half = values[..., half_dim:]
    return jnp.concatenate(
        [first_half * cosine - second_half * sine, second_half * cosine + first_half * sine],
        axis=-1,
    )


def prefill_full(q_heads, key_old, value_old, key_new, value_new, start_at):
    old_len = key_old.shape[0]
    fresh_rows = q_heads.shape[0]
    factor = q_heads.shape[-1] ** (-0.5)
    all_keys = jnp.concatenate([key_old, key_new], axis=0)
    all_values = jnp.concatenate([value_old, value_new], axis=0)
    scores = (
        jnp.einsum("cgd,kd->gck", q_heads, all_keys, preferred_element_type=jnp.float32) * factor
    )
    key_index = jnp.arange(old_len + fresh_rows, dtype=jnp.int32)[None, :]
    row_index = jnp.arange(fresh_rows, dtype=jnp.int32)[:, None]
    allowed = jnp.where(key_index < old_len, key_index < start_at, key_index - old_len <= row_index)
    scores = jnp.where(allowed[None], scores, NEG)
    row_peak = jnp.max(scores, axis=-1, keepdims=True)
    expd = jnp.exp(scores - row_peak)
    weights = (expd / jnp.sum(expd, axis=-1, keepdims=True)).astype(jnp.bfloat16)
    return jnp.einsum(
        "gck,kd->cgd", weights, all_values, preferred_element_type=jnp.float32
    ).astype(jnp.bfloat16)


def decode_attend(q_heads, key_old, value_old, key_self, value_self, lengths):
    factor = q_heads.shape[-1] ** (-0.5)
    past = jnp.einsum("bgd,bld->bgl", q_heads, key_old, preferred_element_type=jnp.float32) * factor
    slot_index = jnp.arange(key_old.shape[1], dtype=jnp.int32)
    past = jnp.where(slot_index[None, None, :] < lengths[:, None, None], past, NEG)
    own_score = (
        jnp.einsum("bgd,bd->bg", q_heads, key_self, preferred_element_type=jnp.float32) * factor
    )
    row_peak = jnp.maximum(jnp.max(past, axis=-1), own_score)
    past_exp = jnp.exp(past - row_peak[..., None])
    own_exp = jnp.exp(own_score - row_peak)
    row_total = jnp.sum(past_exp, axis=-1) + own_exp
    past_w = (past_exp / row_total[..., None]).astype(jnp.bfloat16)
    own_w = (own_exp / row_total).astype(jnp.bfloat16)
    summed = jnp.einsum("bgl,bld->bgd", past_w, value_old, preferred_element_type=jnp.float32)
    summed = (
        summed + own_w.astype(jnp.float32)[..., None] * value_self.astype(jnp.float32)[:, None, :]
    )
    return summed.astype(jnp.bfloat16)


def regroup(rows_in):
    return lax.all_to_all(rows_in, ("req", "kv"), split_axis=0, concat_axis=0, tiled=True)


def shards(
    hidden_in,
    slot_tokens,
    cache_len,
    prefill_start,
    key_cache,
    value_cache,
    key_prefix,
    value_prefix,
    attn_gain,
    q_proj,
    k_proj,
    v_proj,
    q_gain,
    k_gain,
    o_proj,
    ffn_gain,
    w_gate,
    w_up,
    w_down,
    final_gain,
    lm_head,
):
    req_count = lax.axis_size("req")
    kv_count = lax.axis_size("kv")
    devices = req_count * kv_count
    rows_dev = hidden_in.shape[0]
    kv_index = lax.axis_index("kv")
    self_index = lax.axis_index("req") * kv_count + kv_index
    slot_table = slot_tokens.reshape(devices, rows_dev)
    from_self = slot_table // rows_dev == self_index
    send_rows = jnp.sum(jnp.where(from_self, slot_table - self_index * rows_dev, 0), axis=1)
    slot_place = lax.dynamic_index_in_dim(slot_table, self_index, 0, keepdims=False) // rows_dev
    arrived = regroup(hidden_in[send_rows])
    owner_rows = arrived[slot_place]
    rows_all = lax.all_gather(owner_rows, "kv", axis=0, tiled=True)
    normed = norm_rows(rows_all, attn_gain).astype(jnp.bfloat16)
    o_full = lax.all_gather(o_proj, "kv", axis=0, tiled=True)
    ff_dev = w_gate.shape[1]
    ff_piece = ff_dev // kv_count
    gate_w = lax.all_gather(
        lax.dynamic_slice_in_dim(w_gate, kv_index * ff_piece, ff_piece, axis=1),
        "req",
        axis=1,
        tiled=True,
    )
    up_w = lax.all_gather(
        lax.dynamic_slice_in_dim(w_up, kv_index * ff_piece, ff_piece, axis=1),
        "req",
        axis=1,
        tiled=True,
    )
    down_w = lax.all_gather(
        lax.dynamic_slice_in_dim(w_down, kv_index * ff_piece, ff_piece, axis=0),
        "req",
        axis=0,
        tiled=True,
    )
    q_cols = q_proj.shape[1]
    kv_cols = k_proj.shape[1]
    projected = jnp.concatenate(
        [
            jnp.dot(normed, q_proj, preferred_element_type=jnp.float32),
            jnp.dot(normed, k_proj, preferred_element_type=jnp.float32),
            jnp.dot(normed, v_proj, preferred_element_type=jnp.float32),
        ],
        axis=1,
    )
    tok_req = projected.shape[0]
    head_dim = q_gain.shape[0]
    dec_count = cache_len.shape[0]
    fresh_count = tok_req - dec_count
    q_raw = projected[:, :q_cols].reshape(tok_req, q_cols // head_dim, head_dim)
    k_raw = projected[:, q_cols : q_cols + kv_cols].reshape(tok_req, kv_cols // head_dim, head_dim)
    v_new = (
        projected[:, q_cols + kv_cols :]
        .astype(jnp.bfloat16)
        .reshape(tok_req, kv_cols // head_dim, head_dim)
    )
    places = jnp.concatenate(
        [prefill_start[0] + jnp.arange(fresh_count, dtype=jnp.int32), cache_len]
    ).astype(jnp.float32)
    queries = rotate(norm_rows(q_raw, q_gain), places).astype(jnp.bfloat16)
    keys_new = rotate(norm_rows(k_raw, k_gain), places).astype(jnp.bfloat16)
    pre_out = prefill_full(
        queries[:fresh_count],
        key_prefix[0, :, 0:head_dim],
        value_prefix[0, :, 0:head_dim],
        keys_new[:fresh_count, 0],
        v_new[:fresh_count, 0],
        prefill_start[0],
    )
    dec_out = decode_attend(
        queries[fresh_count:],
        key_cache,
        value_cache,
        keys_new[fresh_count:, 0],
        v_new[fresh_count:, 0],
        cache_len,
    )
    pieces = jnp.concatenate([pre_out, dec_out], axis=0)
    pieces, gate_w, up_w, down_w = lax.optimization_barrier((pieces, gate_w, up_w, down_w))
    attended = lax.all_gather(pieces.reshape(tok_req, q_cols), "kv", axis=1, tiled=True)
    resid = (
        rows_all.astype(jnp.float32) + jnp.dot(attended, o_full, preferred_element_type=jnp.float32)
    ).astype(jnp.bfloat16)
    ffn_in = norm_rows(resid, ffn_gain).astype(jnp.bfloat16)
    gate_part = jnp.dot(ffn_in, gate_w, preferred_element_type=jnp.float32)
    up_part = jnp.dot(ffn_in, up_w, preferred_element_type=jnp.float32)
    hidden_act = (jax.nn.silu(gate_part) * up_part).astype(jnp.bfloat16)
    down_part = jnp.dot(hidden_act, down_w, preferred_element_type=jnp.float32)
    ffn_part = lax.psum_scatter(down_part, "kv", scatter_dimension=0, tiled=True)
    mine = lax.dynamic_slice_in_dim(resid, kv_index * rows_dev, rows_dev, axis=0)
    out_rows = (mine.astype(jnp.float32) + ffn_part).astype(jnp.bfloat16)
    going_back = jnp.zeros_like(out_rows).at[slot_place].set(out_rows)
    returned = regroup(going_back)
    layer_out = jnp.zeros_like(hidden_in).at[send_rows].set(returned)
    tail_sum = lax.psum(down_part[fresh_count - 1 :], "kv")
    tail_out = (resid[fresh_count - 1 :].astype(jnp.float32) + tail_sum).astype(jnp.bfloat16)
    tail_rows = norm_rows(tail_out, final_gain).astype(jnp.bfloat16)
    local_peaks = jnp.max(
        jnp.dot(
            lax.all_gather(tail_rows, "req", axis=0, tiled=True),
            lm_head,
            preferred_element_type=jnp.float32,
        ),
        axis=1,
    )
    max_logit = lax.pmax(local_peaks, ("req", "kv"))
    return (layer_out, max_logit)


def solution(mesh):
    placed = (
        P(("req", "kv"), None),
        P(),
        P("req"),
        P("req"),
        P("req", None, "kv"),
        P("req", None, "kv"),
        P("req", None, "kv"),
        P("req", None, "kv"),
        P(),
        P(None, "kv"),
        P(None, "kv"),
        P(None, "kv"),
        P(),
        P(),
        P("kv", None),
        P(),
        P(None, "req"),
        P(None, "req"),
        P("req", None),
        P(),
        P(None, ("req", "kv")),
    )
    return jax.shard_map(
        shards, mesh=mesh, in_specs=placed, out_specs=(P(("req", "kv"), None), P()), check_vma=False
    )
```

profile of v0, /device:TPU:1, one launch (start us, length us, event | category | flops | bytes accessed | tf_op | source)
XLA Modules:
  0.0 573.7 jit_solution(5138658079195809557)
XLA Ops:
  7.2 1.1 select_reduce_fusion
  8.3 2.6 gather_fusion
  11.4 1.0 reduce.2
  12.4 1.2 reshape.450
  13.5 11.5 %all-to-all-start = ((bf16[128,2,1024]{2,1,0:T(2,128)(2,1)}), bf16[128,2,1024]{2,1,0:T(2,128)(2,1)S(1)}, u32[]{:S(2)}, u32[]{:S(2)}) async-start(bf16[128,2,1024]{2,1,0:T(2,128)(2,1)} %reshape.450), calls=%async_computation | async-start | bytes 1048576 | tf_op jit(solution)/shard_map/all_to_all | solution.py:77
  25.8 13.0 %all-to-all-done = bf16[128,2,1024]{2,1,0:T(2,128)(2,1)S(1)} async-done(((bf16[128,2,1024]{2,1,0:T(2,128)(2,1)}), bf16[128,2,1024]{2,1,0:T(2,128)(2,1)S(1)}, u32[]{:S(2)}, u32[]{:S(2)}) %all-to-all-start) | async-done | bytes 524320 | tf_op jit(solution)/shard_map/all_to_all | solution.py:77
  39.5 1.7 gather_fusion.1
  41.6 0.9 copy.60
  42.5 1.5 constant_dynamic-slice_fusion.1
  44.0 0.9 copy.61
  44.9 1.6 constant_dynamic-slice_fusion
  48.5 1.9 multiply_cosine_fusion
  50.5 4.0 fusion.4
  54.5 15.7 %all-gather.19.cloned.1.call-done = bf16[1024,2048]{1,0:T(8,128)(2,1)} async-done(((bf16[128,2048]{1,0:T(8,128)(2,1)}), bf16[1024,2048]{1,0:T(8,128)(2,1)}) %all-gather.19.cloned.1.call-update) | async-done | bytes 4194320 | tf_op jit(solution)/shard_map/all_gather | solution.py:115
  70.1 3.2 fusion.10
  73.6 1.0 fusion.12
  74.8 2.3 multiply_reduce_fusion
  77.1 1.6 copy.48
  78.7 3.7 multiply_reduce_fusion.1
  82.6 1.3 fusion.39
  85.1 1.1 copy-done.4
  86.3 1.3 fusion.77
  88.2 3.6 convolution_convert_fusion
  92.6 15.9 %fusion.78 = (f32[2,1016]{1,0:T(2,128)S(1)}, f32[2,1016,3064]{2,1,0:T(8,128)}) fusion(pred[1016,3064]{1,0:T(8,128)(4,1)} %fusion.4, bf16[1016,128]{1,0:T(8,128)(2,1)S(1)} %copy.47, bf16[2048,128]{1,0:T(8,128)(2,1)S(1)} %bitcast.93, bf16[1024,2,64]{2,0,1:T(8,128)(2,1)S(1)} %get-tuple-element.10, bf16[1024,2,64]{2,0,1:T(8,128)(2,1)S(1)} %get-tuple-element.11), kind=kOutput, calls=%fused_computation.144 | convolution fusion | flops 1621384704 | bytes 29334016 | tf_op jit(solution)/shard_map/sub | solution.py:48
  108.5 12.0 %fusion.18 = bf16[1016,2,128]{2,0,1:T(8,128)(2,1)S(1)} fusion(f32[2,1016,3064]{2,1,0:T(8,128)} %get-tuple-element.25, f32[2,1016]{1,0:T(2,128)S(1)} %get-tuple-element.24, bf16[1016,128]{1,0:T(8,128)(2,1)S(1)} %slice.54, bf16[2048,128]{1,0:T(8,128)(2,1)S(1)} %bitcast.94), kind=kOutput, calls=%fused_computation.32 | convolution fusion | flops 1608149248 | bytes 26216896 | tf_op jit(solution)/shard_map/gck,kd->cgd/dot_general | solution.py:50
  120.6 48.2 %all-gather.11.cloned.1.call-done = bf16[2048,768]{0,1:T(8,128)(2,1)} async-done(((bf16[2048,48]{0,1:T(8,128)(2,1)}), bf16[2048,768]{0,1:T(8,128)(2,1)}) %all-gather.11.cloned.1.call-update) | async-done | bytes 3145744 | tf_op jit(solution)/shard_map/all_gather | solution.py:126
  168.8 48.9 %all-gather.13.cloned.1.call-done = bf16[768,2048]{1,0:T(8,128)(2,1)} async-done(((bf16[48,2048]{1,0:T(8,128)(2,1)}), bf16[768,2048]{1,0:T(8,128)(2,1)}) %all-gather.13.cloned.1.call-update) | async-done | bytes 3145744 | tf_op jit(solution)/shard_map/all_gather | solution.py:132
  217.7 1.0 copy.54
  218.8 49.7 %all-gather.17.cloned.1.call-done = bf16[2048,2048]{1,0:T(8,128)(2,1)} async-done(((bf16[256,2048]{1,0:T(8,128)(2,1)}), bf16[2048,2048]{1,0:T(8,128)(2,1)}) %all-gather.17.cloned.1.call-update) | async-done | bytes 8388624 | tf_op jit(solution)/shard_map/all_gather | solution.py:117
  268.5 34.4 %all-gather.15.cloned.1.call-done = bf16[1024,2048]{0,1:T(8,128)(2,1)} async-done(((bf16[1024,256]{0,1:T(8,128)(2,1)}), bf16[1024,2048]{0,1:T(8,128)(2,1)}) %all-gather.15.cloned.1.call-update) | async-done | bytes 4194320 | tf_op jit(solution)/shard_map/all_gather | solution.py:182
  302.9 14.2 %fusion.7 = (f32[1024]{0:T(1024)S(1)}, bf16[1024,2048]{1,0:T(8,128)(2,1)S(1)}) fusion(bf16[1024,2048]{0,1:T(8,128)(2,1)} %all-gather.15.cloned.1.call-done, bf16[2048,2048]{1,0:T(8,128)(2,1)} %all-gather.17.cloned.1.call-done, bf16[1024,2048]{1,0:T(8,128)(2,1)} %all-gather.19.cloned.1.call-done), kind=kOutput, calls=%fused_computation.20 | convolution fusion | flops 8602516480 | bytes 20975616 | tf_op jit(solution)/shard_map/dot_general | solution.py:184
  317.1 1.9 copy-done.7
  319.0 7.1 %fusion.20 = f32[1024,768]{1,0:T(8,128)} fusion(bf16[2048,768]{0,1:T(8,128)(2,1)} %all-gather.9.cloned.1.call-done, bf16[1024,2048]{1,0:T(8,128)(2,1)S(1)} %get-tuple-element.27, f32[2048]{0:T(1024)S(1)} %copy-done.17, f32[1024]{0:T(1024)S(1)} %add_rsqrt_fusion.1), kind=kOutput, calls=%fused_computation.33 | convolution fusion | flops 3229614080 | bytes 10498048 | tf_op jit(solution)/shard_map/dot_general | solution.py:187
  326.2 14.1 %fusion.23 = f32[1024,2048]{1,0:T(8,128)} fusion(bf16[768,2048]{1,0:T(8,128)(2,1)} %all-gather.13.cloned.1.call-done, f32[1024,768]{1,0:T(8,128)} %fusion.20, bf16[2048,768]{0,1:T(8,128)(2,1)} %all-gather.11.cloned.1.call-done, bf16[1024,2048]{1,0:T(8,128)(2,1)} %copy-done.7, f32[2048]{0:T(1024)S(1)} %copy-done.17, f32[1024]{0:T(1024)S(1)} %add_rsqrt_fusion.1), kind=kOutput, calls=%fused_computation.34 | convolution fusion | flops 6455558144 | bytes 22032384 | tf_op jit(solution)/shard_map/dot_general | solution.py:190
  340.2 1.6 slice.65
  342.6 56.0 %all-reduce.2.cloned.1.call-done = f32[9,2048]{1,0:T(8,128)} async-done(((f32[9,2048]{1,0:T(8,128)}), f32[9,2048]{1,0:T(8,128)}) %all-reduce.2.cloned.1.call-update) | async-done | bytes 73744 | tf_op jit(solution)/shard_map/psum | solution.py:197
  398.6 1.0 fusion.44
  399.6 1.0 fusion.51
  400.6 53.5 %reduce-scatter.2.cloned.1.call-done = f32[128,2048]{1,0:T(8,128)} async-done(((f32[1024,2048]{1,0:T(8,128)}), f32[128,2048]{1,0:T(8,128)}) %reduce-scatter.2.cloned.1.call-update) | async-done | bytes 1048592 | tf_op jit(solution)/shard_map/reduce_scatter | solution.py:191
  454.1 2.6 scatter_custom_fusion
  456.7 1.0 reduce.3
  457.7 1.2 reshape.452
  458.9 8.4 %all-to-all-start.1 = ((bf16[128,2,1024]{2,1,0:T(2,128)(2,1)}), bf16[128,2,1024]{2,1,0:T(2,128)(2,1)S(1)}, u32[]{:S(2)}, u32[]{:S(2)}) async-start(bf16[128,2,1024]{2,1,0:T(2,128)(2,1)} %reshape.452), calls=%async_computation.2 | async-start | bytes 1048576 | tf_op jit(solution)/shard_map/all_to_all | solution.py:77
  467.3 22.4 %all-gather.1 = bf16[16,9,2048]{2,1,0:T(8,128)(2,1)S(1)} all-gather(bf16[1,9,2048]{2,1,0:T(8,128)(2,1)S(1)} %fusion.51), channel_id=1, replica_groups=mesh['req'=16,'kv'=8] {'req'}, dimensions={0}, use_global_device_ids=true | all-gather | bytes 626688 | tf_op jit(solution)/shard_map/all_gather | solution.py:202
  489.7 1.1 reshape.441
  490.8 4.4 convolution_reduce_fusion
  495.2 68.5 %pmax.7 = f32[144]{0:T(256)} all-reduce(f32[144]{0:T(256)S(1)} %convolution_reduce_fusion), channel_id=1, replica_groups=mesh['req'=16,'kv'=8] {'req','kv'}, use_global_device_ids=true, to_apply=%region_15.16 | all-reduce | flops 144 | bytes 1152 | tf_op jit(solution)/shard_map/pmax | solution.py:208
  564.2 2.4 scatter_custom_fusion.1
  (90 shorter events, 8.3 us)
Async XLA Ops:
  7.2 34.2 %copy-start = (bf16[2048,384]{1,0:T(8,128)(2,1)S(1)}, bf16[2048,384]{1,0:T(8,128)(2,1)}, u32[]{:S(2)}) copy-start(bf16[2048,384]{1,0:T(8,128)(2,1)} %param.37) | copy-start | bytes 4718596
  13.5 25.2 %all-to-all-start = ((bf16[128,2,1024]{2,1,0:T(2,128)(2,1)}), bf16[128,2,1024]{2,1,0:T(2,128)(2,1)S(1)}, u32[]{:S(2)}, u32[]{:S(2)}) async-start(bf16[128,2,1024]{2,1,0:T(2,128)(2,1)} %reshape.450), calls=%async_computation | async-start | bytes 1048576 | tf_op jit(solution)/shard_map/all_to_all | solution.py:77
  25.0 45.1 %all-gather.19.cloned.1.call-start = ((), (), s32[]{:S(2)}) async-start(), calls=%async_computation.10 | async-start | bytes 4718592 | tf_op jit(solution)/shard_map/all_gather | solution.py:115
  41.2 7.1 %copy-start.10 = (s32[8]{0:T(128)S(1)}, s32[8]{0:T(128)}, u32[]{:S(2)}) copy-start(s32[8]{0:T(128)} %param.23) | copy-start | bytes 100
  41.3 79.3 %all-gather.9.cloned.1.call-start = ((), (), s32[]{:S(2)}) async-start(), calls=%async_computation.3 | async-start | bytes 3342336 | tf_op jit(solution)/shard_map/all_gather | solution.py:120
  42.5 126.3 %all-gather.11.cloned.1.call-start = ((), (), s32[]{:S(2)}) async-start(), calls=%async_computation.4 | async-start | bytes 3342336 | tf_op jit(solution)/shard_map/all_gather | solution.py:126
  44.8 172.8 %all-gather.13.cloned.1.call-start = ((), (), s32[]{:S(2)}) async-start(), calls=%async_computation.5 | async-start | bytes 3342336 | tf_op jit(solution)/shard_map/all_gather | solution.py:132
  46.5 221.9 %all-gather.17.cloned.1.call-start = ((), (), s32[]{:S(2)}) async-start(), calls=%async_computation.7 | async-start | bytes 9437184 | tf_op jit(solution)/shard_map/all_gather | solution.py:117
  47.1 255.8 %all-gather.15.cloned.1.call-start = ((), (), s32[]{:S(2)}) async-start(), calls=%async_computation.6 | async-start | bytes 4718592 | tf_op jit(solution)/shard_map/all_gather | solution.py:182
  48.5 24.9 %copy-start.8 = (f32[2048]{0:T(1024)S(1)}, f32[2048]{0:T(1024)}, u32[]{:S(2)}) copy-start(f32[2048]{0:T(1024)} %param.29) | copy-start | bytes 24580
  70.1 3.4 copy-start.2
  73.6 1.2 copy-start.13
  74.8 2.3 copy-start.3
  74.8 3.9 copy-start.6
  77.1 5.3 copy-start.11
  78.7 5.4 copy-start.12
  84.1 2.2 copy-start.4
  84.9 3.2 copy-start.14
  88.1 3.7 copy-start.5
  88.2 4.5 copy-start.15
  92.6 15.9 %copy-start.16 = (bf16[1,2048,128]{2,1,0:T(8,128)(2,1)S(1)}, bf16[1,2048,128]{2,1,0:T(8,128)(2,1)}, u32[]{:S(2)}) copy-start(bf16[1,2048,128]{2,1,0:T(8,128)(2,1)} %param.28) | copy-start | bytes 1572868
  218.7 100.3 %copy-start.17 = (f32[2048]{0:T(1024)S(1)}, f32[2048]{0:T(1024)}, u32[]{:S(2)}) copy-start(f32[2048]{0:T(1024)} %param.36) | copy-start | bytes 24580
  218.7 179.8 %all-reduce.2.cloned.1.call-start = ((), (), s32[]{:S(2)}) async-start(), calls=%async_computation.9 | async-start | bytes 262144 | tf_op jit(solution)/shard_map/psum | solution.py:197
  317.1 1.9 copy-start.7
  341.8 57.8 %copy-start.9 = (f32[2048]{0:T(1024)S(1)}, f32[2048]{0:T(1024)}, u32[]{:S(2)}) copy-start(f32[2048]{0:T(1024)} %param.40) | copy-start | bytes 24580
  341.8 112.3 %reduce-scatter.2.cloned.1.call-start = ((), (), s32[]{:S(2)}) async-start(), calls=%async_computation.8 | async-start | bytes 9437184 | tf_op jit(solution)/shard_map/reduce_scatter | solution.py:191
  458.9 104.8 %all-to-all-start.1 = ((bf16[128,2,1024]{2,1,0:T(2,128)(2,1)}), bf16[128,2,1024]{2,1,0:T(2,128)(2,1)S(1)}, u32[]{:S(2)}, u32[]{:S(2)}) async-start(bf16[128,2,1024]{2,1,0:T(2,128)(2,1)} %reshape.452), calls=%async_computation.2 | async-start | bytes 1048576 | tf_op jit(solution)/shard_map/all_to_all | solution.py:77
  489.7 76.9 %copy-start.1 = (bf16[2048,384]{1,0:T(8,128)(2,1)S(1)}, bf16[2048,384]{1,0:T(8,128)(2,1)}, u32[]{:S(2)}) copy-start(bf16[2048,384]{1,0:T(8,128)(2,1)} %param.37) | copy-start | bytes 4718596
Sparse Core Ops, SparseCore 0:
  41.4 28.7 all-gather.18
  72.3 47.3 all-gather.8
  121.8 46.8 all-gather.10
  170.8 46.8 all-gather.12
  219.2 49.1 all-gather.16
  270.6 32.2 all-gather.14
  341.9 56.5 all-reduce.1
  401.1 52.9 reduce-scatter.1
where the time goes:
time: 578 us; the launch traced here: 574 us
  waiting for transfers between devices  321 us (56%)
  blocking collectives  90.9 us (16%)
  matrix products  79.3 us (14%)
  local copies, waits for them, and re-layouts  24.9 us (4%)
  other arithmetic  21.6 us (4%)
  starting transfers between devices  20.8 us (4%)
  between operations  15.5 us (3%)
    pmax x1, blocking collectives, shards(): max_logit = lax.pmax(local_peaks, ('req', 'kv'))  68.5 us
    psum x1, waiting for transfers between devices, shards(): tail_sum = lax.psum(down_part[fresh_count - 1:], 'kv')  56 us
    reduce_scatter x1, waiting for transfers between devices, shards(): lax.psum_scatter(down_part, 'kv', scatter_dimension=0, tiled=True)  53.5 us
    all_gather x1, waiting for transfers between devices, shards(): o_full = lax.all_gather(o_proj, 'kv', axis=0, tiled=True)  49.7 us
    all_gather x1, waiting for transfers between devices, shards(): lax.all_gather(lax.dynamic_slice_in_dim(w_down, kv_index * ff_piece, ff_p...  48.9 us
    all_gather x1, waiting for transfers between devices, shards(): lax.all_gather(lax.dynamic_slice_in_dim(w_up, kv_index * ff_piece, ff_pie...  48.2 us
    all_gather x1, waiting for transfers between devices, shards(): lax.all_gather(pieces.reshape(tok_req, q_cols), 'kv', axis=1, tiled=True)  34.4 us
    all_gather x1, blocking collectives, shards(): lax.all_gather(tail_rows, 'req', axis=0, tiled=True)  22.4 us
  transfers between devices with their start and end apart: 10, of which 8 were waited for; matrix products, arithmetic and copies ran while one was open for 12% of the time, Pallas kernels for 0%

commit v1 on v0

--- a/solution.py
+++ b/solution.py
@@ -123,12 +123,9 @@
         axis=1,
         tiled=True,
     )
-    up_w = lax.all_gather(
-        lax.dynamic_slice_in_dim(w_up, kv_index * ff_piece, ff_piece, axis=1),
-        "req",
-        axis=1,
-        tiled=True,
-    )
+    x = lax.dynamic_slice_in_dim(w_up, kv_index * ff_piece, ff_piece, axis=1)
+    stack = jnp.stack([x] * lax.axis_size("req"))
+    up_w = jnp.concatenate(lax.all_to_all(stack, "req", 0, 0), axis=1)
     down_w = lax.all_gather(
         lax.dynamic_slice_in_dim(w_down, kv_index * ff_piece, ff_piece, axis=0),
         "req",

time: 578 us -> 539 us (0.933)
  waiting for transfers between devices: 321 us -> 276 us
    all_gather x1 -> x0, waiting for transfers between devices: 48.2 us -> none  [shards(): lax.all_gather(lax.dynamic_slice_in_dim(w_up, kv_index * ff_piece, ff_pie...]
    all_gather x1, waiting for transfers between devices: 0.02 us -> 10.3 us  [shards(): lax.all_gather(lax.dynamic_slice_in_dim(w_gate, kv_index * ff_piece, ff_p...]
    all_gather x1, waiting for transfers between devices: 15.7 us -> 8.8 us  [shards(): rows_all = lax.all_gather(owner_rows, 'kv', axis=0, tiled=True)]
  transfers between devices with their start and end apart: 10 -> 10, of which waited for: 8 -> 8; matrix products, arithmetic and copies ran while one was open for 12% -> 13% of each run, Pallas kernels for 0% -> 0%
where the time goes in v1:
time: 539 us; the launch traced here: 534 us
  waiting for transfers between devices  276 us (51%)
  blocking collectives  91 us (17%)
  matrix products  78.5 us (15%)
  starting transfers between devices  25.2 us (5%)
  local copies, waits for them, and re-layouts  24.5 us (5%)
  other arithmetic  23.8 us (4%)
  between operations  15.5 us (3%)
    pmax x1, blocking collectives, shards(): max_logit = lax.pmax(local_peaks, ('req', 'kv'))  68.6 us
    psum x1, waiting for transfers between devices, shards(): tail_sum = lax.psum(down_part[fresh_count - 1:], 'kv')  56 us
    reduce_scatter x1, waiting for transfers between devices, shards(): lax.psum_scatter(down_part, 'kv', scatter_dimension=0, tiled=True)  53.5 us
    all_gather x1, waiting for transfers between devices, shards(): o_full = lax.all_gather(o_proj, 'kv', axis=0, tiled=True)  49.7 us
    all_gather x1, waiting for transfers between devices, shards(): lax.all_gather(lax.dynamic_slice_in_dim(w_down, kv_index * ff_piece, ff_p...  49.1 us
    all_gather x1, waiting for transfers between devices, shards(): lax.all_gather(pieces.reshape(tok_req, q_cols), 'kv', axis=1, tiled=True)  34.4 us
    all_gather x1, blocking collectives, shards(): lax.all_gather(tail_rows, 'req', axis=0, tiled=True)  22.4 us
    all_to_all x2, starting transfers between devices, regroup(): lax.all_to_all(rows_in, ('req', 'kv'), split_axis=0, concat_axis=0, tiled...  19.9 us
  transfers between devices with their start and end apart: 10, of which 8 were waited for; matrix products, arithmetic and copies ran while one was open for 13% of the time, Pallas kernels for 0%

profile of v1, /device:TPU:1, one launch (start us, length us, event | category | flops | bytes accessed | tf_op | source)
XLA Modules:
  0.0 534.4 jit_solution(5312094007408343566)
XLA Ops:
  7.2 1.1 select_reduce_fusion
  8.3 2.6 gather_fusion
  11.4 1.0 reduce.2
  12.4 1.2 reshape.460
  13.5 11.5 %all-to-all-start = ((bf16[128,2,1024]{2,1,0:T(2,128)(2,1)}), bf16[128,2,1024]{2,1,0:T(2,128)(2,1)S(1)}, u32[]{:S(2)}, u32[]{:S(2)}) async-start(bf16[128,2,1024]{2,1,0:T(2,128)(2,1)} %reshape.460), calls=%async_computation | async-start | bytes 1048576 | tf_op jit(solution)/shard_map/all_to_all | solution.py:77
  25.8 13.0 %all-to-all-done = bf16[128,2,1024]{2,1,0:T(2,128)(2,1)S(1)} async-done(((bf16[128,2,1024]{2,1,0:T(2,128)(2,1)}), bf16[128,2,1024]{2,1,0:T(2,128)(2,1)S(1)}, u32[]{:S(2)}, u32[]{:S(2)}) %all-to-all-start) | async-done | bytes 524320 | tf_op jit(solution)/shard_map/all_to_all | solution.py:77
  39.5 1.7 gather_fusion.1
  41.6 0.9 copy.61
  42.5 1.6 constant_dynamic-slice_fusion
  44.7 1.5 constant_dynamic-slice_fusion.1
  46.4 2.0 stack.2
  48.4 4.5 all-to-all-start.1
  54.3 3.0 multiply_cosine_fusion
  57.3 4.0 fusion.4
  61.3 8.8 %all-gather.16.cloned.1.call-done = bf16[1024,2048]{1,0:T(8,128)(2,1)} async-done(((bf16[128,2048]{1,0:T(8,128)(2,1)}), bf16[1024,2048]{1,0:T(8,128)(2,1)}) %all-gather.16.cloned.1.call-update) | async-done | bytes 4194320 | tf_op jit(solution)/shard_map/all_gather | solution.py:115
  70.1 3.2 fusion.10
  73.6 1.0 fusion.12
  74.8 1.3 multiply_reduce_fusion
  77.1 3.7 multiply_reduce_fusion.1
  81.0 1.2 fusion.39
  82.7 1.7 subtract_convert_fusion
  84.7 1.3 fusion.77
  86.6 3.6 convolution_convert_fusion
  91.0 16.0 %fusion.78 = (f32[2,1016]{1,0:T(2,128)S(1)}, f32[2,1016,3064]{2,1,0:T(8,128)}) fusion(pred[1016,3064]{1,0:T(8,128)(4,1)} %fusion.4, bf16[1016,128]{1,0:T(8,128)(2,1)S(1)} %copy.48, bf16[2048,128]{1,0:T(8,128)(2,1)S(1)} %bitcast.96, bf16[1024,2,64]{2,0,1:T(8,128)(2,1)S(1)} %get-tuple-element.10, bf16[1024,2,64]{2,0,1:T(8,128)(2,1)S(1)} %get-tuple-element.11), kind=kOutput, calls=%fused_computation.144 | convolution fusion | flops 1621384704 | bytes 29334016 | tf_op jit(solution)/shard_map/sub | solution.py:48
  107.0 12.0 %fusion.18 = bf16[1016,2,128]{2,0,1:T(8,128)(2,1)S(1)} fusion(f32[2,1016,3064]{2,1,0:T(8,128)} %get-tuple-element.25, f32[2,1016]{1,0:T(2,128)S(1)} %get-tuple-element.24, bf16[1016,128]{1,0:T(8,128)(2,1)S(1)} %slice.54, bf16[2048,128]{1,0:T(8,128)(2,1)} %bitcast.97), kind=kOutput, calls=%fused_computation.32 | convolution fusion | flops 1608149248 | bytes 26216896 | tf_op jit(solution)/shard_map/gck,kd->cgd/dot_general | solution.py:50
  119.1 10.3 %all-gather.8.cloned.1.call-done = bf16[2048,768]{0,1:T(8,128)(2,1)} async-done(((bf16[2048,48]{0,1:T(8,128)(2,1)}), bf16[2048,768]{0,1:T(8,128)(2,1)}) %all-gather.8.cloned.1.call-update) | async-done | bytes 3145744 | tf_op jit(solution)/shard_map/all_gather | solution.py:120
  129.4 49.1 %all-gather.10.cloned.1.call-done = bf16[768,2048]{1,0:T(8,128)(2,1)} async-done(((bf16[48,2048]{1,0:T(8,128)(2,1)}), bf16[768,2048]{1,0:T(8,128)(2,1)}) %all-gather.10.cloned.1.call-update) | async-done | bytes 3145744 | tf_op jit(solution)/shard_map/all_gather | solution.py:129
  178.4 1.0 copy.55
  179.5 49.7 %all-gather.14.cloned.1.call-done = bf16[2048,2048]{1,0:T(8,128)(2,1)} async-done(((bf16[256,2048]{1,0:T(8,128)(2,1)}), bf16[2048,2048]{1,0:T(8,128)(2,1)}) %all-gather.14.cloned.1.call-update) | async-done | bytes 8388624 | tf_op jit(solution)/shard_map/all_gather | solution.py:117
  229.2 34.4 %all-gather.12.cloned.1.call-done = bf16[1024,2048]{0,1:T(8,128)(2,1)} async-done(((bf16[1024,256]{0,1:T(8,128)(2,1)}), bf16[1024,2048]{0,1:T(8,128)(2,1)}) %all-gather.12.cloned.1.call-update) | async-done | bytes 4194320 | tf_op jit(solution)/shard_map/all_gather | solution.py:179
  263.6 14.2 %fusion.7 = (f32[1024]{0:T(1024)S(1)}, bf16[1024,2048]{1,0:T(8,128)(2,1)S(1)}) fusion(bf16[1024,2048]{0,1:T(8,128)(2,1)} %all-gather.12.cloned.1.call-done, bf16[2048,2048]{1,0:T(8,128)(2,1)} %all-gather.14.cloned.1.call-done, bf16[1024,2048]{1,0:T(8,128)(2,1)} %all-gather.16.cloned.1.call-done), kind=kOutput, calls=%fused_computation.20 | convolution fusion | flops 8602516480 | bytes 20975616 | tf_op jit(solution)/shard_map/dot_general | solution.py:181
  277.9 1.9 copy-done.7
  279.8 7.1 %fusion.20 = f32[1024,768]{1,0:T(8,128)} fusion(bf16[2048,768]{0,1:T(8,128)(2,1)} %all-gather.8.cloned.1.call-done, bf16[1024,2048]{1,0:T(8,128)(2,1)S(1)} %get-tuple-element.27, f32[2048]{0:T(1024)S(1)} %copy-done.16, f32[1024]{0:T(1024)S(1)} %add_rsqrt_fusion.1), kind=kOutput, calls=%fused_computation.33 | convolution fusion | flops 3229614080 | bytes 10498048 | tf_op jit(solution)/shard_map/dot_general | solution.py:184
  286.9 14.1 %fusion.23 = f32[1024,2048]{1,0:T(8,128)} fusion(bf16[768,2048]{1,0:T(8,128)(2,1)} %all-gather.10.cloned.1.call-done, f32[1024,768]{1,0:T(8,128)} %fusion.20, bf16[2048,768]{0,1:T(8,128)(2,1)} %bitcast.21, bf16[1024,2048]{1,0:T(8,128)(2,1)} %copy-done.7, f32[2048]{0:T(1024)S(1)} %copy-done.16, f32[1024]{0:T(1024)S(1)} %add_rsqrt_fusion.1), kind=kOutput, calls=%fused_computation.34 | convolution fusion | flops 6455558144 | bytes 22032384 | tf_op jit(solution)/shard_map/dot_general | solution.py:187
  301.0 1.6 slice.65
  303.4 56.0 %all-reduce.2.cloned.1.call-done = f32[9,2048]{1,0:T(8,128)} async-done(((f32[9,2048]{1,0:T(8,128)}), f32[9,2048]{1,0:T(8,128)}) %all-reduce.2.cloned.1.call-update) | async-done | bytes 73744 | tf_op jit(solution)/shard_map/psum | solution.py:194
  359.3 1.0 fusion.44
  360.4 1.0 fusion.51
  361.4 53.5 %reduce-scatter.2.cloned.1.call-done = f32[128,2048]{1,0:T(8,128)} async-done(((f32[1024,2048]{1,0:T(8,128)}), f32[128,2048]{1,0:T(8,128)}) %reduce-scatter.2.cloned.1.call-update) | async-done | bytes 1048592 | tf_op jit(solution)/shard_map/reduce_scatter | solution.py:188
  414.9 2.6 scatter_custom_fusion
  417.5 1.0 reduce.3
  418.5 1.2 reshape.462
  419.6 8.4 %all-to-all-start.2 = ((bf16[128,2,1024]{2,1,0:T(2,128)(2,1)}), bf16[128,2,1024]{2,1,0:T(2,128)(2,1)S(1)}, u32[]{:S(2)}, u32[]{:S(2)}) async-start(bf16[128,2,1024]{2,1,0:T(2,128)(2,1)} %reshape.462), calls=%async_computation.3 | async-start | bytes 1048576 | tf_op jit(solution)/shard_map/all_to_all | solution.py:77
  428.1 22.4 %all-gather.1 = bf16[16,9,2048]{2,1,0:T(8,128)(2,1)S(1)} all-gather(bf16[1,9,2048]{2,1,0:T(8,128)(2,1)S(1)} %fusion.51), channel_id=1, replica_groups=mesh['req'=16,'kv'=8] {'req'}, dimensions={0}, use_global_device_ids=true | all-gather | bytes 626688 | tf_op jit(solution)/shard_map/all_gather | solution.py:199
  450.5 1.1 reshape.451
  451.5 4.4 convolution_reduce_fusion
  455.9 68.6 %pmax.7 = f32[144]{0:T(256)} all-reduce(f32[144]{0:T(256)S(1)} %convolution_reduce_fusion), channel_id=1, replica_groups=mesh['req'=16,'kv'=8] {'req','kv'}, use_global_device_ids=true, to_apply=%region_15.16 | all-reduce | flops 144 | bytes 1152 | tf_op jit(solution)/shard_map/pmax | solution.py:205
  524.9 2.4 scatter_custom_fusion.1
  (88 shorter events, 8.9 us)
Async XLA Ops:
  7.2 34.2 %copy-start = (bf16[2048,384]{1,0:T(8,128)(2,1)S(1)}, bf16[2048,384]{1,0:T(8,128)(2,1)}, u32[]{:S(2)}) copy-start(bf16[2048,384]{1,0:T(8,128)(2,1)} %param.37) | copy-start | bytes 4718596
  13.5 25.2 %all-to-all-start = ((bf16[128,2,1024]{2,1,0:T(2,128)(2,1)}), bf16[128,2,1024]{2,1,0:T(2,128)(2,1)S(1)}, u32[]{:S(2)}, u32[]{:S(2)}) async-start(bf16[128,2,1024]{2,1,0:T(2,128)(2,1)} %reshape.460), calls=%async_computation | async-start | bytes 1048576 | tf_op jit(solution)/shard_map/all_to_all | solution.py:77
  25.0 45.1 %all-gather.16.cloned.1.call-start = ((), (), s32[]{:S(2)}) async-start(), calls=%async_computation.10 | async-start | bytes 4718592 | tf_op jit(solution)/shard_map/all_gather | solution.py:115
  41.3 88.1 %all-gather.8.cloned.1.call-start = ((), (), s32[]{:S(2)}) async-start(), calls=%async_computation.4 | async-start | bytes 3342336 | tf_op jit(solution)/shard_map/all_gather | solution.py:120
  42.5 136.0 %all-gather.10.cloned.1.call-start = ((), (), s32[]{:S(2)}) async-start(), calls=%async_computation.5 | async-start | bytes 3342336 | tf_op jit(solution)/shard_map/all_gather | solution.py:129
  44.1 185.1 %all-gather.14.cloned.1.call-start = ((), (), s32[]{:S(2)}) async-start(), calls=%async_computation.7 | async-start | bytes 9437184 | tf_op jit(solution)/shard_map/all_gather | solution.py:117
  46.4 7.8 %copy-start.10 = (s32[8]{0:T(128)S(1)}, s32[8]{0:T(128)}, u32[]{:S(2)}) copy-start(s32[8]{0:T(128)} %param.23) | copy-start | bytes 100
  48.4 70.7 %all-to-all-start.1 = ((bf16[16,2048,48]{1,2,0:T(8,128)(2,1)}), bf16[16,2048,48]{1,2,0:T(8,128)(2,1)}, u32[]{:S(2)}, u32[]{:S(2)}) async-start(bf16[16,2048,48]{1,2,0:T(8,128)(2,1)} %stack.2), calls=%async_computation.1 | async-start | bytes 6291456 | tf_op jit(solution)/shard_map/all_to_all | solution.py:128
  52.9 210.7 %all-gather.12.cloned.1.call-start = ((), (), s32[]{:S(2)}) async-start(), calls=%async_computation.6 | async-start | bytes 4718592 | tf_op jit(solution)/shard_map/all_gather | solution.py:179
  54.3 19.1 %copy-start.8 = (f32[2048]{0:T(1024)S(1)}, f32[2048]{0:T(1024)}, u32[]{:S(2)}) copy-start(f32[2048]{0:T(1024)} %param.29) | copy-start | bytes 24580
  70.1 3.4 copy-start.2
  73.6 1.2 copy-start.13
  74.8 1.9 copy-start.3
  74.8 2.3 copy-start.6
  76.7 4.1 copy-start.11
  77.1 5.2 copy-start.12
  82.3 2.4 copy-start.4
  84.4 2.2 copy-start.14
  86.6 3.7 copy-start.5
  86.6 4.5 copy-start.15
  179.5 100.3 %copy-start.16 = (f32[2048]{0:T(1024)S(1)}, f32[2048]{0:T(1024)}, u32[]{:S(2)}) copy-start(f32[2048]{0:T(1024)} %param.36) | copy-start | bytes 24580
  179.5 179.8 %all-reduce.2.cloned.1.call-start = ((), (), s32[]{:S(2)}) async-start(), calls=%async_computation.9 | async-start | bytes 262144 | tf_op jit(solution)/shard_map/psum | solution.py:194
  277.8 2.0 copy-start.7
  302.6 57.8 %copy-start.9 = (f32[2048]{0:T(1024)S(1)}, f32[2048]{0:T(1024)}, u32[]{:S(2)}) copy-start(f32[2048]{0:T(1024)} %param.40) | copy-start | bytes 24580
  302.6 112.3 %reduce-scatter.2.cloned.1.call-start = ((), (), s32[]{:S(2)}) async-start(), calls=%async_computation.8 | async-start | bytes 9437184 | tf_op jit(solution)/shard_map/reduce_scatter | solution.py:188
  419.6 104.8 %all-to-all-start.2 = ((bf16[128,2,1024]{2,1,0:T(2,128)(2,1)}), bf16[128,2,1024]{2,1,0:T(2,128)(2,1)S(1)}, u32[]{:S(2)}, u32[]{:S(2)}) async-start(bf16[128,2,1024]{2,1,0:T(2,128)(2,1)} %reshape.462), calls=%async_computation.3 | async-start | bytes 1048576 | tf_op jit(solution)/shard_map/all_to_all | solution.py:77
  450.5 76.9 %copy-start.1 = (bf16[2048,384]{1,0:T(8,128)(2,1)S(1)}, bf16[2048,384]{1,0:T(8,128)(2,1)}, u32[]{:S(2)}) copy-start(bf16[2048,384]{1,0:T(8,128)(2,1)} %param.37) | copy-start | bytes 4718596
Sparse Core Ops, SparseCore 0:
  41.4 28.7 all-gather.15
  72.3 57.0 all-gather.7
  131.5 46.8 all-gather.9
  180.0 49.1 all-gather.13
  231.3 32.2 all-gather.11
  302.7 56.5 all-reduce.1
  361.8 52.9 reduce-scatter.1
